TPU v7x, 512 devices: a whole 4x4x16 slice. The times are simulated.
512 devices in a mesh: cell: 32 (over x, y, core), blk: 16 (over z).
Axes of the slice: x: 4, y: 4, z: 16, core: 2. Of those that a mesh axis runs over, the one named last changes fastest.
Arguments:
- snapshots: float32 [512, 65536], P('blk', 'cell'), may hold values from -100 to 100
- plan: int32 [31, 32], replicated, may hold values from 0 to 31, as said below
Outputs:
- energy_field: float32 [512, 65536], P('blk', 'cell')
- mode_energy: float32 [512], P('blk')
Inputs may be any that keep to these rules, and one draw needn't show every extreme that they name: `plan`: each row pairs every index 0 .. 31 with exactly one other index (the partner's partner is the index itself, never the index), and over all rows every two indices are paired exactly once.
All inputs are finite; a program needn't handle non-finite values.
Results may differ from a plain program's by a relative error of at most 0.0055.
Values sent between devices are 32-bit elements; how exact they have to be, the bound alone decides.
A program may use at most 64 MiB of HBM per device.

v0:
```python
import jax
import jax.numpy as jnp
from jax import lax
from jax.sharding import PartitionSpec as P

ROUNDS = 7


def passed_along(value, axis, steps):
    count = lax.axis_size(axis)
    first, last = (max(0, -steps), min(count, count - steps))
    return lax.ppermute(value, axis, [(source, source + steps) for source in range(first, last)])


def inner_sweep(gram_whole, plan):
    pair_width = gram_whole.shape[0]
    positions = jnp.arange(pair_width, dtype=jnp.int32)

    def one_step(step_index, loop_state):
        gram_now, accumulated = loop_state
        partner = lax.dynamic_index_in_dim(plan, step_index, 0, keepdims=False)
        onehot = (partner[:, None] == positions[None, :]).astype(jnp.float32)
        symmetric = 0.5 * (gram_now + gram_now.T)
        own_diag = jnp.diagonal(symmetric)
        cross_term = jnp.sum(onehot * symmetric, axis=1)
        other_diag = jnp.sum(onehot * own_diag[None, :], axis=1)
        is_lower = positions < partner
        spread = jnp.where(is_lower, own_diag - other_diag, other_diag - own_diag)
        angles = 0.5 * jnp.arctan2(2.0 * cross_term, spread)
        cosine = jnp.cos(angles)
        sine_part = jnp.where(is_lower, jnp.sin(angles), -jnp.sin(angles))
        rotation_step = jnp.diag(cosine) + (onehot * sine_part[:, None]).T
        gram_now = jnp.dot(
            jnp.dot(rotation_step.T, gram_now, precision=lax.Precision.HIGHEST),
            rotation_step,
            precision=lax.Precision.HIGHEST,
        )
        accumulated = jnp.dot(accumulated, rotation_step, precision=lax.Precision.HIGHEST)
        return (gram_now, accumulated)

    initial = (gram_whole, jnp.eye(pair_width, dtype=jnp.float32))
    return lax.fori_loop(0, pair_width - 1, one_step, initial)[1]


def self_gram(block):
    return jnp.dot(block, block.T, precision=lax.Precision.HIGHEST)


def on_device(snapshots, plan):
    pair_width = snapshots.shape[0]
    half_width = pair_width // 2
    local_rows = snapshots.shape[1]
    block_devices = lax.axis_size("blk")
    position = lax.axis_index("blk")

    def round_step(round_index, loop_state):
        current, gram_local = loop_state
        gram_whole = lax.psum(gram_local, "cell")
        turning = inner_sweep(gram_whole, plan)
        rotated = jnp.dot(turning.T, current, precision=lax.Precision.HIGHEST)
        upper_part = rotated[:half_width]
        lower_part = rotated[half_width:]
        rightward = jnp.where(position == 0, lower_part, upper_part)
        from_left = passed_along(rightward, "blk", 1)
        from_right = passed_along(lower_part, "blk", -1)
        new_upper = jnp.where(position == 0, upper_part, from_left)
        new_lower = jnp.where(position == block_devices - 1, upper_part, from_right)
        current = jnp.concatenate([new_upper, new_lower], axis=0)
        gram_local = self_gram(current)
        return (current, gram_local)

    gram_first = self_gram(snapshots)
    current, gram_local = lax.fori_loop(0, ROUNDS, round_step, (snapshots, gram_first))
    squared = current * current
    energy_local = jnp.sum(squared, axis=1)
    total_rows = local_rows * lax.axis_size("cell")
    mode_energy = lax.psum(energy_local, "cell") / total_rows
    return (squared, mode_energy)


def solution(mesh):
    return jax.shard_map(
        on_device,
        mesh=mesh,
        in_specs=(P("blk", "cell"), P()),
        out_specs=(P("blk", "cell"), P("blk")),
        check_vma=False,
    )
```

profile of v0, /device:TPU:1, one launch (start us, length us, event | category | flops | bytes accessed | tf_op | source)
XLA Modules:
  0.0 1892.4 jit_solution(1336124570133756698)
XLA Ops:
  1.9 1820.3 %while.37 = (s32[]{:T(128)}, f32[32,2048]{1,0:T(8,128)S(1)}, f32[32,32]{1,0:T(8,128)S(1)}, pred[]{:T(512)}, s32[31,32]{1,0:T(8,128)}, /*index=5*/pred[]{:T(512)}, s32[]{:T(128)}, s32[]{:T(128)}, s32[]{:T(128)}) while((s32[]{:T(128)}, f32[32,2048]{1,0:T(8,128)S(1)}, f32[32,32]{1,0:T(8,128)S(1)}, pred[]{:T(512)}, s32[31,32]{1,0:T(8,128)}, ...), condition=%wide.region_6.7_spmd, body=%wide.region_0.6_spmd.sunk | while | flops 51701092 | bytes 3620785 | solution.py:73
  2.0 125.0 %psum.18 = f32[32,32]{1,0:T(8,128)S(1)} all-reduce(f32[32,32]{1,0:T(8,128)S(1)} %get-tuple-element.345), channel_id=1, replica_groups=mesh['cell'=32,'blk'=16] {'cell'}, use_global_device_ids=true, to_apply=%region_1.0 | all-reduce | flops 1024 | bytes 8192 | tf_op jit(solution)/shard_map/while/body/eval_jaxpr/psum | solution.py:58
  126.9 124.2 %while.38 = (s32[]{:T(128)}, f32[32,32]{1,0:T(8,128)S(1)}, f32[32,32]{0,1:T(8,128)S(1)}, s32[31,32]{1,0:T(8,128)}, s32[]{:T(128)}) while((s32[]{:T(128)}, f32[32,32]{1,0:T(8,128)S(1)}, f32[32,32]{0,1:T(8,128)S(1)}, s32[31,32]{1,0:T(8,128)}, s32[]{:T(128)}) %tuple.77), condition=%wide.region_5.5_spmd.clone.clone, body=%wide.region_2.4_spmd.clone.clone.sunk | while | flops 1202530 | bytes 61137 | solution.py:42
  260.6 125.0 %psum.18 = f32[32,32]{1,0:T(8,128)S(1)} all-reduce(f32[32,32]{1,0:T(8,128)S(1)} %get-tuple-element.345), channel_id=1, replica_groups=mesh['cell'=32,'blk'=16] {'cell'}, use_global_device_ids=true, to_apply=%region_1.0 | all-reduce | flops 1024 | bytes 8192 | tf_op jit(solution)/shard_map/while/body/eval_jaxpr/psum | solution.py:58
  385.6 124.2 %while.38 = (s32[]{:T(128)}, f32[32,32]{1,0:T(8,128)S(1)}, f32[32,32]{0,1:T(8,128)S(1)}, s32[31,32]{1,0:T(8,128)}, s32[]{:T(128)}) while((s32[]{:T(128)}, f32[32,32]{1,0:T(8,128)S(1)}, f32[32,32]{0,1:T(8,128)S(1)}, s32[31,32]{1,0:T(8,128)}, s32[]{:T(128)}) %tuple.77), condition=%wide.region_5.5_spmd.clone.clone, body=%wide.region_2.4_spmd.clone.clone.sunk | while | flops 1202530 | bytes 61137 | solution.py:42
  515.7 5.1 collective-permute-done.1
  521.2 124.9 %psum.18 = f32[32,32]{1,0:T(8,128)S(1)} all-reduce(f32[32,32]{1,0:T(8,128)S(1)} %get-tuple-element.345), channel_id=1, replica_groups=mesh['cell'=32,'blk'=16] {'cell'}, use_global_device_ids=true, to_apply=%region_1.0 | all-reduce | flops 1024 | bytes 8192 | tf_op jit(solution)/shard_map/while/body/eval_jaxpr/psum | solution.py:58
  646.1 124.2 %while.38 = (s32[]{:T(128)}, f32[32,32]{1,0:T(8,128)S(1)}, f32[32,32]{0,1:T(8,128)S(1)}, s32[31,32]{1,0:T(8,128)}, s32[]{:T(128)}) while((s32[]{:T(128)}, f32[32,32]{1,0:T(8,128)S(1)}, f32[32,32]{0,1:T(8,128)S(1)}, s32[31,32]{1,0:T(8,128)}, s32[]{:T(128)}) %tuple.77), condition=%wide.region_5.5_spmd.clone.clone, body=%wide.region_2.4_spmd.clone.clone.sunk | while | flops 1202530 | bytes 61137 | solution.py:42
  770.7 4.9 collective-permute-start
  777.5 4.1 collective-permute-done.1
  782.0 124.9 %psum.18 = f32[32,32]{1,0:T(8,128)S(1)} all-reduce(f32[32,32]{1,0:T(8,128)S(1)} %get-tuple-element.345), channel_id=1, replica_groups=mesh['cell'=32,'blk'=16] {'cell'}, use_global_device_ids=true, to_apply=%region_1.0 | all-reduce | flops 1024 | bytes 8192 | tf_op jit(solution)/shard_map/while/body/eval_jaxpr/psum | solution.py:58
  906.9 124.2 %while.38 = (s32[]{:T(128)}, f32[32,32]{1,0:T(8,128)S(1)}, f32[32,32]{0,1:T(8,128)S(1)}, s32[31,32]{1,0:T(8,128)}, s32[]{:T(128)}) while((s32[]{:T(128)}, f32[32,32]{1,0:T(8,128)S(1)}, f32[32,32]{0,1:T(8,128)S(1)}, s32[31,32]{1,0:T(8,128)}, s32[]{:T(128)}) %tuple.77), condition=%wide.region_5.5_spmd.clone.clone, body=%wide.region_2.4_spmd.clone.clone.sunk | while | flops 1202530 | bytes 61137 | solution.py:42
  1041.4 125.0 %psum.18 = f32[32,32]{1,0:T(8,128)S(1)} all-reduce(f32[32,32]{1,0:T(8,128)S(1)} %get-tuple-element.345), channel_id=1, replica_groups=mesh['cell'=32,'blk'=16] {'cell'}, use_global_device_ids=true, to_apply=%region_1.0 | all-reduce | flops 1024 | bytes 8192 | tf_op jit(solution)/shard_map/while/body/eval_jaxpr/psum | solution.py:58
  1166.4 124.2 %while.38 = (s32[]{:T(128)}, f32[32,32]{1,0:T(8,128)S(1)}, f32[32,32]{0,1:T(8,128)S(1)}, s32[31,32]{1,0:T(8,128)}, s32[]{:T(128)}) while((s32[]{:T(128)}, f32[32,32]{1,0:T(8,128)S(1)}, f32[32,32]{0,1:T(8,128)S(1)}, s32[31,32]{1,0:T(8,128)}, s32[]{:T(128)}) %tuple.77), condition=%wide.region_5.5_spmd.clone.clone, body=%wide.region_2.4_spmd.clone.clone.sunk | while | flops 1202530 | bytes 61137 | solution.py:42
  1291.0 4.5 collective-permute-start
  1297.4 4.1 collective-permute-done.1
  1301.9 124.9 %psum.18 = f32[32,32]{1,0:T(8,128)S(1)} all-reduce(f32[32,32]{1,0:T(8,128)S(1)} %get-tuple-element.345), channel_id=1, replica_groups=mesh['cell'=32,'blk'=16] {'cell'}, use_global_device_ids=true, to_apply=%region_1.0 | all-reduce | flops 1024 | bytes 8192 | tf_op jit(solution)/shard_map/while/body/eval_jaxpr/psum | solution.py:58
  1426.8 124.2 %while.38 = (s32[]{:T(128)}, f32[32,32]{1,0:T(8,128)S(1)}, f32[32,32]{0,1:T(8,128)S(1)}, s32[31,32]{1,0:T(8,128)}, s32[]{:T(128)}) while((s32[]{:T(128)}, f32[32,32]{1,0:T(8,128)S(1)}, f32[32,32]{0,1:T(8,128)S(1)}, s32[31,32]{1,0:T(8,128)}, s32[]{:T(128)}) %tuple.77), condition=%wide.region_5.5_spmd.clone.clone, body=%wide.region_2.4_spmd.clone.clone.sunk | while | flops 1202530 | bytes 61137 | solution.py:42
  1551.4 4.9 collective-permute-start
  1558.2 4.1 collective-permute-done.1
  1562.7 124.9 %psum.18 = f32[32,32]{1,0:T(8,128)S(1)} all-reduce(f32[32,32]{1,0:T(8,128)S(1)} %get-tuple-element.345), channel_id=1, replica_groups=mesh['cell'=32,'blk'=16] {'cell'}, use_global_device_ids=true, to_apply=%region_1.0 | all-reduce | flops 1024 | bytes 8192 | tf_op jit(solution)/shard_map/while/body/eval_jaxpr/psum | solution.py:58
  1687.6 124.2 %while.38 = (s32[]{:T(128)}, f32[32,32]{1,0:T(8,128)S(1)}, f32[32,32]{0,1:T(8,128)S(1)}, s32[31,32]{1,0:T(8,128)}, s32[]{:T(128)}) while((s32[]{:T(128)}, f32[32,32]{1,0:T(8,128)S(1)}, f32[32,32]{0,1:T(8,128)S(1)}, s32[31,32]{1,0:T(8,128)}, s32[]{:T(128)}) %tuple.77), condition=%wide.region_5.5_spmd.clone.clone, body=%wide.region_2.4_spmd.clone.clone.sunk | while | flops 1202530 | bytes 61137 | solution.py:42
  1817.7 4.1 collective-permute-done.1
  1823.1 68.8 %psum.16 = f32[32]{0:T(128)S(1)} all-reduce(f32[32]{0:T(128)S(1)} %get-tuple-element.224), channel_id=1, replica_groups=mesh['cell'=32,'blk'=16] {'cell'}, use_global_device_ids=true, to_apply=%region_8.9 | all-reduce | flops 32 | bytes 256 | tf_op jit(solution)/shard_map/psum | solution.py:77
  (2670 shorter events, 900.3 us)
Async XLA Ops:
  251.5 4.7 collective-permute-start
  254.3 5.9 collective-permute-start.1
  510.2 5.5 collective-permute-start
  513.8 7.0 collective-permute-start.1
  770.7 6.8 collective-permute-start
  775.5 6.0 collective-permute-start.1
  1031.4 5.6 collective-permute-start
  1035.1 5.9 collective-permute-start.1
  1291.0 6.4 collective-permute-start
  1295.5 6.0 collective-permute-start.1
  1551.4 6.8 collective-permute-start
  1556.2 6.0 collective-permute-start.1
  1812.2 5.6 collective-permute-start
  1815.8 6.0 collective-permute-start.1
where the time goes:
time: 1920 us; the launch traced here: 1890 us
  blocking collectives  943 us (49%)
  other arithmetic  370 us (19%)
  local copies, waits for them, and re-layouts  324 us (17%)
  matrix products  171 us (9%)
  starting transfers between devices  36.9 us (2%)
  waiting for transfers between devices  33.7 us (2%)
    psum x7, blocking collectives, round_step(): gram_whole = lax.psum(gram_local, 'cell')  875 us
    cos x217, other arithmetic, one_step(): cosine = jnp.cos(angles)  167 us
    select_n x217, other arithmetic, one_step(): sine_part = jnp.where(is_lower, jnp.sin(angles), -jnp.sin(angles))  159 us
    gather x217, local copies, waits for them, and re-layouts, one_step(): own_diag = jnp.diagonal(symmetric)  156 us
    eq x217, local copies, waits for them, and re-layouts, one_step(): onehot = (partner[:, None] == positions[None, :]).astype(jnp.float32)  151 us
    psum x1, blocking collectives, on_device(): mode_energy = lax.psum(energy_local, 'cell') / total_rows  68.8 us
    dot_general x217, matrix products, one_step(): jnp.dot(accumulated, rotation_step, precision=lax.Precision.HIGHEST)  60.8 us
    dot_general x217, matrix products, one_step(): jnp.dot(rotation_step.T, gram_now, precision=lax.Precision.HIGHEST)  60.1 us
  transfers between devices with their start and end apart: 14, of which 14 were waited for; matrix products, arithmetic and copies ran while one was open for 0% of the time, Pallas kernels for 0%

commit v1 on v0

v1 whole, which is shorter than its diff:
```python
import functools

import jax
import jax.numpy as jnp
from jax import lax
from jax.experimental import pallas as pl
from jax.experimental.pallas import tpu as pltpu
from jax.sharding import PartitionSpec as P

ROUNDS = 7
INNER = 8
WIDTH = 32
HALF = 16
LANES = 128
MESH = pl.DeviceIdType.MESH
HIGHEST = lax.Precision.HIGHEST


def turn_of(own, other, cross, lower):
    difference = own - other
    spread = jnp.where(lower, difference, -difference)
    height = 2.0 * cross
    size = jnp.maximum(jnp.abs(height), jnp.abs(spread))
    nothing = size == 0.0
    factor = pl.reciprocal(jnp.where(nothing, 1.0, size), approx=True)
    y = height * factor
    d = jnp.where(nothing, 1.0, spread * factor)
    inverse = lax.rsqrt(y * y + d * d)
    half_up = 0.5 + 0.5 * jnp.abs(d) * inverse
    root = lax.rsqrt(half_up)
    large = half_up * root
    small = 0.5 * jnp.abs(y) * inverse * root
    ahead = d >= 0.0
    cosine = jnp.where(ahead, large, small)
    sine = jnp.where(ahead, small, large)
    sine = jnp.where(y < 0.0, -sine, sine)
    return cosine, jnp.where(lower, sine, -sine)


def permuted(value, index):
    return jnp.take_along_axis(value, index, axis=1, mode="promise_in_bounds")


def sweep(gram, plan_ref):
    shape = (WIDTH, LANES)
    row = lax.broadcasted_iota(jnp.int32, shape, 0)
    lane = lax.broadcasted_iota(jnp.int32, shape, 1)
    own_mask = row == lane
    lane_row = lax.broadcasted_iota(jnp.int32, (1, LANES), 1)

    def step(k, state):
        gram, turning = state
        partner = plan_ref[pl.ds(k, 1), :]
        index = jnp.broadcast_to(partner, shape)
        partner_mask = row == index
        crossed = permuted(gram, index)
        own = jnp.sum(jnp.where(own_mask, gram, 0.0), axis=0, keepdims=True)
        cross = jnp.sum(jnp.where(own_mask, crossed, 0.0), axis=0, keepdims=True)
        other = jnp.sum(jnp.where(partner_mask, crossed, 0.0), axis=0, keepdims=True)
        cosine, sine = turn_of(own, other, cross, lane_row < partner)
        half_done = gram * cosine + crossed * sine
        flipped = half_done.T[:WIDTH]
        flipped = jnp.concatenate([flipped, jnp.zeros((WIDTH, LANES - WIDTH), jnp.float32)], axis=1)
        gram = flipped * cosine + permuted(flipped, index) * sine
        turning = turning * cosine + permuted(turning, index) * sine
        return gram, turning

    start = jnp.where(own_mask, 1.0, 0.0).astype(jnp.float32)
    return lax.fori_loop(0, WIDTH - 1, step, (gram, start))[1]


def kernel(groups, blocks, snap_ref, plan_ref, out_ref, mode_ref,
           current, rotated, inner_slots, outer_slots,
           inner_send, inner_recv, outer_send, outer_recv, move_send, move_recv):
    cell = lax.axis_index("cell")
    pair = lax.axis_index("blk")
    inner = lax.rem(cell, INNER)
    outer = cell // INNER
    base = outer * INNER

    def inner_peer(offset):
        return lax.rem(inner + offset, INNER)

    def outer_peer(offset):
        return lax.rem(outer + offset, groups)

    barrier = pltpu.get_barrier_semaphore()
    for offset in range(1, INNER):
        pl.semaphore_signal(barrier, inc=1, device_id=(base + inner_peer(offset), pair), device_id_type=MESH)
    for offset in range(1, groups):
        pl.semaphore_signal(barrier, inc=1, device_id=(outer_peer(offset) * INNER + inner, pair), device_id_type=MESH)

    for step in (1, blocks - 1):
        pl.semaphore_signal(barrier, inc=1, device_id=(cell, lax.rem(pair + step, blocks)), device_id_type=MESH)
    pl.semaphore_wait(barrier, INNER - 1 + groups - 1 + 2)

    def inner_copy(slot, whose, peer, offset):
        return pltpu.make_async_remote_copy(
            src_ref=inner_slots.at[slot, whose], dst_ref=inner_slots.at[slot, whose],
            send_sem=inner_send.at[slot, offset], recv_sem=inner_recv.at[slot, whose],
            device_id=(base + peer, pair), device_id_type=MESH)

    def outer_copy(slot, whose, peer, offset):
        return pltpu.make_async_remote_copy(
            src_ref=outer_slots.at[slot, whose], dst_ref=outer_slots.at[slot, whose],
            send_sem=outer_send.at[slot, offset], recv_sem=outer_recv.at[slot, whose],
            device_id=(peer * INNER + inner, pair), device_id_type=MESH)

    def summed_gram(slot):
        block = current[slot].reshape(WIDTH, -1)
        gram = lax.dot_general(block, block, (((1,), (1,)), ((), ())), precision=HIGHEST,
                               preferred_element_type=jnp.float32)
        packed = jnp.concatenate([gram[8 * i:8 * i + 8] for i in range(4)], axis=1)
        inner_slots[slot, inner] = packed
        for offset in range(1, INNER):
            inner_copy(slot, inner, inner_peer(offset), offset).start()
        for offset in range(1, INNER):
            inner_copy(slot, inner_peer(offset), inner_peer(offset), offset).wait_recv()
        total = inner_slots[slot, 0]
        for i in range(1, INNER):
            total = total + inner_slots[slot, i]
        outer_slots[slot, outer] = total
        for offset in range(1, groups):
            outer_copy(slot, outer, outer_peer(offset), offset).start()
        for offset in range(1, groups):
            outer_copy(slot, outer_peer(offset), outer_peer(offset), offset).wait_recv()
        total = outer_slots[slot, 0]
        for i in range(1, groups):
            total = total + outer_slots[slot, i]
        for offset in range(1, INNER):
            inner_copy(slot, inner, inner_peer(offset), offset).wait_send()
        for offset in range(1, groups):
            outer_copy(slot, outer, outer_peer(offset), offset).wait_send()
        return jnp.concatenate(
            [total] + [pltpu.roll(total, LANES - WIDTH * i, 1) for i in range(1, 4)], axis=0)

    def right_copy(after):
        return pltpu.make_async_remote_copy(
            src_ref=rotated.at[jnp.where(pair == 0, 1, 0)], dst_ref=current.at[after, 0],
            send_sem=move_send.at[0], recv_sem=move_recv.at[after, 0],
            device_id=(cell, jnp.minimum(pair + 1, blocks - 1)), device_id_type=MESH)

    def left_copy(after):
        return pltpu.make_async_remote_copy(
            src_ref=rotated.at[1], dst_ref=current.at[after, 1],
            send_sem=move_send.at[1], recv_sem=move_recv.at[after, 1],
            device_id=(cell, jnp.maximum(pair - 1, 0)), device_id_type=MESH)

    current[0] = snap_ref[...].reshape(2, HALF, -1)

    def one_round(r, carry):
        now = lax.rem(r, 2)
        after = 1 - now
        turning = sweep(summed_gram(now), plan_ref)
        block = current[now].reshape(WIDTH, -1)
        turned = lax.dot_general(turning[:, :WIDTH], block, (((0,), (0,)), ((), ())), precision=HIGHEST,
                                 preferred_element_type=jnp.float32)
        rotated[...] = turned.reshape(2, HALF, -1)

        @pl.when(pair < blocks - 1)
        def _():
            right_copy(after).start()

        @pl.when(pair > 0)
        def _():
            left_copy(after).start()

        @pl.when(pair == 0)
        def _():
            current[after, 0] = rotated[0]

        @pl.when(pair == blocks - 1)
        def _():
            current[after, 1] = rotated[0]

        @pl.when(pair > 0)
        def _():
            right_copy(after).wait_recv()
            left_copy(after).wait_send()

        @pl.when(pair < blocks - 1)
        def _():
            left_copy(after).wait_recv()
            right_copy(after).wait_send()

        return carry

    lax.fori_loop(0, ROUNDS, one_round, 0)
    last = ROUNDS % 2
    gram = summed_gram(last)
    row = lax.broadcasted_iota(jnp.int32, (WIDTH, LANES), 0)
    lane = lax.broadcasted_iota(jnp.int32, (WIDTH, LANES), 1)
    mode_ref[...] = jnp.sum(jnp.where(row == lane, gram, 0.0), axis=0, keepdims=True)
    out_ref[...] = current[last].reshape(WIDTH, -1)


def on_device(snapshots, plan):
    cells = lax.axis_size("cell")
    blocks = lax.axis_size("blk")
    groups = cells // INNER
    local = snapshots.shape[1]
    steps = plan.shape[0]
    rest = jnp.broadcast_to(jnp.arange(WIDTH, LANES, dtype=jnp.int32), (steps, LANES - WIDTH))
    partners = jnp.concatenate([plan, rest], axis=1)
    field, energy = pl.pallas_call(
        functools.partial(kernel, groups, blocks),
        out_shape=(jax.ShapeDtypeStruct((WIDTH, local), jnp.float32),
                   jax.ShapeDtypeStruct((1, LANES), jnp.float32)),
        in_specs=[pl.BlockSpec(memory_space=pltpu.VMEM)] * 2,
        out_specs=(pl.BlockSpec(memory_space=pltpu.VMEM),) * 2,
        scratch_shapes=[
            pltpu.VMEM((2, 2, HALF, local), jnp.float32),
            pltpu.VMEM((2, HALF, local), jnp.float32),
            pltpu.VMEM((2, INNER, 8, LANES), jnp.float32),
            pltpu.VMEM((2, groups, 8, LANES), jnp.float32),
            pltpu.SemaphoreType.DMA((2, INNER)),
            pltpu.SemaphoreType.DMA((2, INNER)),
            pltpu.SemaphoreType.DMA((2, groups)),
            pltpu.SemaphoreType.DMA((2, groups)),
            pltpu.SemaphoreType.DMA((2,)),
            pltpu.SemaphoreType.DMA((2, 2)),
        ],
        compiler_params=pltpu.CompilerParams(collective_id=0, has_side_effects=True),
        name="rounds",
    )(snapshots, partners)
    return field * field, energy[0, :WIDTH] / (local * cells)


def solution(mesh):
    return jax.shard_map(
        on_device,
        mesh=mesh,
        in_specs=(P("blk", "cell"), P()),
        out_specs=(P("blk", "cell"), P("blk")),
        check_vma=False,
    )
```

time: 1920 us -> 170 us (0.09); the launches traced: 1890 us -> 170 us
  blocking collectives: 943 us -> 0 us
  other arithmetic: 370 us -> 3.61 us
  local copies, waits for them, and re-layouts: 324 us -> 0.08 us
  matrix products: 171 us -> 0 us
  Pallas kernels: 0 us -> 165 us
  starting transfers between devices: 36.9 us -> 0 us
  waiting for transfers between devices: 33.7 us -> 0 us
    psum x8 -> x0, blocking collectives: 943 us -> none  [the longest x7 875 us: round_step(): gram_whole = lax.psum(gram_local, 'cell')]
    dot_general x666 -> x0, matrix products: 171 us -> none  [the longest x217 60.8 us: one_step(): jnp.dot(accumulated, rotation_step, precision=lax.Precision.HIGHEST)]
    cos x217 -> x0, other arithmetic: 167 us -> none  [one_step(): cosine = jnp.cos(angles)]
    pallas_call x0 -> x1, Pallas kernels: none -> 165 us  [on_device(): pl.pallas_call(functools.partial(kernel, groups, blocks), out_shape=(jax....]
    select_n x231 -> x0, other arithmetic: 160 us -> none  [the longest x217 159 us: one_step(): sine_part = jnp.where(is_lower, jnp.sin(angles), -jnp.sin(angles))]
    gather x217 -> x0, local copies, waits for them, and re-layouts: 156 us -> none  [one_step(): own_diag = jnp.diagonal(symmetric)]
    eq x217 -> x0, local copies, waits for them, and re-layouts: 151 us -> none  [one_step(): onehot = (partner[:, None] == positions[None, :]).astype(jnp.float32)]
    reduce_sum x218 -> x0, other arithmetic: 39.8 us -> none  [the longest x217 38.9 us: one_step(): cross_term = jnp.sum(onehot * symmetric, axis=1)]
  transfers between devices with their start and end apart: 14 -> 0, of which waited for: 14 -> 0; matrix products, arithmetic and copies ran while one was open for 0% -> 0% of each run, Pallas kernels for 0% -> 0%
where the time goes in v1:
time: 170 us
  Pallas kernels  165 us (97%)
  other arithmetic  3.61 us (2%)
    pallas_call x1, Pallas kernels, on_device(): pl.pallas_call(functools.partial(kernel, groups, blocks), out_shape=(jax....  165 us

profile of v1, /device:TPU:1, one launch (start us, length us, event | category | flops | bytes accessed | tf_op | source)
XLA Modules:
  0.0 169.5 jit_solution(11424115116152623504)
XLA Ops:
  0.6 0.1 pad.1.clone
  0.7 1.3 pad_add_fusion.plan_ref
  2.0 165.2 %rounds.1 = (f32[32,2048]{1,0:T(8,128)}, f32[1,128]{1,0:T(1,128)}) custom-call(f32[32,2048]{1,0:T(8,128)} %snap_ref.1, s32[31,128]{1,0:T(8,128)} %pad_add_fusion.plan_ref), custom_call_target="tpu_custom_call" | custom-call | tf_op jit(solution)/shard_map/rounds/pallas_call | solution.py:205
  167.3 0.0 copy-start
  167.3 1.8 %mul.3 = f32[32,2048]{1,0:T(8,128)} multiply(f32[32,2048]{1,0:T(8,128)} %get-tuple-element.4, f32[32,2048]{1,0:T(8,128)} %get-tuple-element.4) | non-fusion elementwise | flops 65536 | bytes 786432 | tf_op jit(solution)/shard_map/mul | solution.py:226
  169.0 0.0 copy-done
  169.0 0.5 multiply_bitcast_fusion
  (1 shorter events, 0.0 us)
Async XLA Ops:
  167.3 1.8 %copy-start = (f32[1,128]{1,0:T(1,128)S(1)}, f32[1,128]{1,0:T(1,128)}, u32[]{:S(2)}) copy-start(f32[1,128]{1,0:T(1,128)} %get-tuple-element.5) | copy-start | bytes 1540

commit v2 on v1

v2 whole, which is shorter than its diff:
```python
import functools

import jax
import jax.numpy as jnp
from jax import lax
from jax.experimental import pallas as pl
from jax.experimental.pallas import tpu as pltpu
from jax.sharding import PartitionSpec as P

ROUNDS = 7
INNER = 8
WIDTH = 32
HALF = 16
LANES = 128
CHUNKS = 4
MESH = pl.DeviceIdType.MESH
HIGHEST = lax.Precision.HIGHEST


def turn_of(own, other, cross, lower):
    difference = own - other
    spread = jnp.where(lower, difference, -difference)
    height = 2.0 * cross
    size = jnp.maximum(jnp.abs(height), jnp.abs(spread))
    nothing = size == 0.0
    factor = pl.reciprocal(jnp.where(nothing, 1.0, size), approx=True)
    y = height * factor
    d = jnp.where(nothing, 1.0, spread * factor)
    square = y * y + d * d
    inverse = lax.rsqrt(square)
    inverse = inverse * (1.5 - 0.5 * square * (inverse * inverse))
    half_up = 0.5 + 0.5 * jnp.abs(d) * inverse
    root = lax.rsqrt(half_up)
    large = half_up * root
    small = 0.5 * jnp.abs(y) * inverse * root
    unit = 1.5 - 0.5 * (large * large + small * small)
    large = large * unit
    small = small * unit
    ahead = d >= 0.0
    cosine = jnp.where(ahead, large, small)
    sine = jnp.where(ahead, small, large)
    return cosine, jnp.where((y < 0.0) == lower, -sine, sine)


def permuted(value, index):
    return jnp.take_along_axis(value, index, axis=1, mode="promise_in_bounds")


def sweep(gram, table_ref):
    shape = (WIDTH, LANES)
    row = lax.broadcasted_iota(jnp.int32, shape, 0)
    lane = lax.broadcasted_iota(jnp.int32, shape, 1)
    own_mask = row == lane
    any_own_mask = row == lane % WIDTH
    lane_row = lax.broadcasted_iota(jnp.int32, (1, LANES), 1)

    def at_mask(mask, value):
        return jnp.sum(jnp.where(mask, value, 0.0), axis=0, keepdims=True)

    def to_front(value, group):
        return pltpu.roll(value, LANES - WIDTH * group, 1)

    def step(k, state):
        gram, turning, own, other, cross = state
        table = table_ref[pl.ds(k, 1), :]
        partners = table_ref[pl.ds(k + WIDTH, 1), :]
        index = jnp.broadcast_to(table, shape)
        partner_mask = row == jnp.broadcast_to(partners, shape)
        crossed = permuted(gram, index)
        from_own = at_mask(any_own_mask, crossed)
        from_partner = at_mask(partner_mask, crossed)
        next_row = jnp.broadcast_to(to_front(table, 1), (8, LANES))

        def at_next(value):
            return permuted(jnp.broadcast_to(value, (8, LANES)), next_row)[:1]

        own_q, own_pq = to_front(from_own, 1), to_front(from_own, 2)
        partner_q, partner_pq = to_front(from_partner, 1), to_front(from_partner, 2)
        both_own = 0.5 * (own_q + at_next(own_q))
        both_partner = 0.5 * (partner_pq + at_next(partner_pq))
        ahead = 0.5 * (own_pq + at_next(partner_q))
        behind = 0.5 * (partner_q + at_next(own_pq))
        cosine, sine = turn_of(own, other, cross, lane_row < table)
        cosine_q, sine_q = at_next(cosine), at_next(sine)
        next_own = own + sine * (2.0 * cosine * cross - sine * (own - other))
        next_other = at_next(next_own)
        next_cross = (((cosine * cosine_q) * both_own + (sine * sine_q) * both_partner)
                      + ((cosine * sine_q) * ahead + (sine * cosine_q) * behind))
        half_done = gram * cosine + crossed * sine
        flipped = half_done.T[:WIDTH]
        flipped = jnp.concatenate([flipped, jnp.zeros((WIDTH, LANES - WIDTH), jnp.float32)], axis=1)
        gram = flipped * cosine + permuted(flipped, index) * sine
        turning = turning * cosine + permuted(turning, index) * sine
        return gram, turning, next_own, next_other, next_cross

    start = jnp.where(own_mask, 1.0, 0.0).astype(jnp.float32)
    first = jnp.broadcast_to(table_ref[pl.ds(0, 1), :], shape)
    crossed = permuted(gram, first)
    cross = at_mask(own_mask, crossed)
    cross = 0.5 * (cross + permuted(jnp.broadcast_to(cross, (8, LANES)), first[:8])[:1])
    state = (gram, start, at_mask(own_mask, gram), at_mask(row == first, crossed), cross)
    return lax.fori_loop(0, WIDTH - 1, step, state)[1]


def step_table(plan):
    same = jnp.arange(WIDTH, dtype=jnp.int32)
    following = jnp.concatenate([plan[1:], same[None]], axis=0)
    both = jnp.take_along_axis(plan, following, axis=1)
    still = jnp.broadcast_to(same, plan.shape)
    table = jnp.concatenate([plan, following, both, still], axis=1)
    blank = jnp.zeros((1, LANES), jnp.int32)
    return jnp.concatenate([table, blank, jnp.tile(plan, (1, LANES // WIDTH)), blank], axis=0)


def kernel(groups, blocks, snap_ref, plan_ref, out_ref, mode_ref,
           current, rotated, inner_slots, outer_slots,
           inner_send, inner_recv, outer_send, outer_recv, move_send, move_recv):
    cell = lax.axis_index("cell")
    pair = lax.axis_index("blk")
    inner = lax.rem(cell, INNER)
    outer = cell // INNER
    base = outer * INNER

    def inner_peer(offset):
        return lax.rem(inner + offset, INNER)

    def outer_peer(offset):
        return lax.rem(outer + offset, groups)

    barrier = pltpu.get_barrier_semaphore()
    for offset in range(1, INNER):
        pl.semaphore_signal(barrier, inc=1, device_id=(base + inner_peer(offset), pair), device_id_type=MESH)
    for offset in range(1, groups):
        pl.semaphore_signal(barrier, inc=1, device_id=(outer_peer(offset) * INNER + inner, pair), device_id_type=MESH)

    for step in (1, blocks - 1):
        pl.semaphore_signal(barrier, inc=1, device_id=(cell, lax.rem(pair + step, blocks)), device_id_type=MESH)
    pl.semaphore_wait(barrier, INNER - 1 + groups - 1 + 2)

    def inner_copy(slot, whose, peer, offset):
        return pltpu.make_async_remote_copy(
            src_ref=inner_slots.at[slot, whose], dst_ref=inner_slots.at[slot, whose],
            send_sem=inner_send.at[slot, offset], recv_sem=inner_recv.at[slot, whose],
            device_id=(base + peer, pair), device_id_type=MESH)

    def outer_copy(slot, whose, peer, offset):
        return pltpu.make_async_remote_copy(
            src_ref=outer_slots.at[slot, whose], dst_ref=outer_slots.at[slot, whose],
            send_sem=outer_send.at[slot, offset], recv_sem=outer_recv.at[slot, whose],
            device_id=(peer * INNER + inner, pair), device_id_type=MESH)

    def chunk_gram(slot, chunk):
        block = current[slot, chunk].reshape(WIDTH, -1)
        return lax.dot_general(block, block, (((1,), (1,)), ((), ())), precision=HIGHEST,
                               preferred_element_type=jnp.float32)

    def summed_gram(slot, gram):
        packed = jnp.concatenate([gram[8 * i:8 * i + 8] for i in range(4)], axis=1)
        inner_slots[slot, inner] = packed
        for offset in range(1, INNER):
            inner_copy(slot, inner, inner_peer(offset), offset).start()
        for offset in range(1, INNER):
            inner_copy(slot, inner_peer(offset), inner_peer(offset), offset).wait_recv()
        total = inner_slots[slot, 0]
        for i in range(1, INNER):
            total = total + inner_slots[slot, i]
        outer_slots[slot, outer] = total
        for offset in range(1, groups):
            outer_copy(slot, outer, outer_peer(offset), offset).start()
        for offset in range(1, groups):
            outer_copy(slot, outer_peer(offset), outer_peer(offset), offset).wait_recv()
        total = outer_slots[slot, 0]
        for i in range(1, groups):
            total = total + outer_slots[slot, i]
        for offset in range(1, INNER):
            inner_copy(slot, inner, inner_peer(offset), offset).wait_send()
        for offset in range(1, groups):
            outer_copy(slot, outer, outer_peer(offset), offset).wait_send()
        return jnp.concatenate(
            [total] + [pltpu.roll(total, LANES - WIDTH * i, 1) for i in range(1, 4)], axis=0)

    def right_copy(after, chunk):
        return pltpu.make_async_remote_copy(
            src_ref=rotated.at[chunk, jnp.where(pair == 0, 1, 0)], dst_ref=current.at[after, chunk, 0],
            send_sem=move_send.at[0, chunk], recv_sem=move_recv.at[after, 0, chunk],
            device_id=(cell, jnp.minimum(pair + 1, blocks - 1)), device_id_type=MESH)

    def left_copy(after, chunk):
        return pltpu.make_async_remote_copy(
            src_ref=rotated.at[chunk, 1], dst_ref=current.at[after, chunk, 1],
            send_sem=move_send.at[1, chunk], recv_sem=move_recv.at[after, 1, chunk],
            device_id=(cell, jnp.maximum(pair - 1, 0)), device_id_type=MESH)

    width = current.shape[-1]
    first_gram = jnp.zeros((WIDTH, WIDTH), jnp.float32)
    for chunk in range(CHUNKS):
        current[0, chunk] = snap_ref[:, chunk * width:(chunk + 1) * width].reshape(2, HALF, width)
        first_gram = first_gram + chunk_gram(0, chunk)

    def one_round(r, gram):
        now = lax.rem(r, 2)
        after = 1 - now
        turning = sweep(summed_gram(now, gram), plan_ref)[:, :WIDTH]
        for chunk in range(CHUNKS):
            block = current[now, chunk].reshape(WIDTH, width)
            turned = lax.dot_general(turning, block, (((0,), (0,)), ((), ())), precision=HIGHEST,
                                     preferred_element_type=jnp.float32)
            rotated[chunk] = turned.reshape(2, HALF, width)

            @pl.when(pair < blocks - 1)
            def _():
                right_copy(after, chunk).start()

            @pl.when(pair > 0)
            def _():
                left_copy(after, chunk).start()

        @pl.when(pair == 0)
        def _():
            for chunk in range(CHUNKS):
                current[after, chunk, 0] = rotated[chunk, 0]

        @pl.when(pair == blocks - 1)
        def _():
            for chunk in range(CHUNKS):
                current[after, chunk, 1] = rotated[chunk, 0]

        gram = jnp.zeros((WIDTH, WIDTH), jnp.float32)
        for chunk in range(CHUNKS):
            @pl.when(pair > 0)
            def _():
                right_copy(after, chunk).wait_recv()

            @pl.when(pair < blocks - 1)
            def _():
                left_copy(after, chunk).wait_recv()

            gram = gram + chunk_gram(after, chunk)

        for chunk in range(CHUNKS):
            @pl.when(pair > 0)
            def _():
                left_copy(after, chunk).wait_send()

            @pl.when(pair < blocks - 1)
            def _():
                right_copy(after, chunk).wait_send()

        return gram

    gram = lax.fori_loop(0, ROUNDS, one_round, first_gram)
    last = ROUNDS % 2
    gram = summed_gram(last, gram)
    row = lax.broadcasted_iota(jnp.int32, (WIDTH, LANES), 0)
    lane = lax.broadcasted_iota(jnp.int32, (WIDTH, LANES), 1)
    mode_ref[...] = jnp.sum(jnp.where(row == lane, gram, 0.0), axis=0, keepdims=True)
    for chunk in range(CHUNKS):
        out_ref[:, chunk * width:(chunk + 1) * width] = current[last, chunk].reshape(WIDTH, width)


def on_device(snapshots, plan):
    cells = lax.axis_size("cell")
    blocks = lax.axis_size("blk")
    groups = cells // INNER
    local = snapshots.shape[1]
    field, energy = pl.pallas_call(
        functools.partial(kernel, groups, blocks),
        out_shape=(jax.ShapeDtypeStruct((WIDTH, local), jnp.float32),
                   jax.ShapeDtypeStruct((1, LANES), jnp.float32)),
        in_specs=[pl.BlockSpec(memory_space=pltpu.VMEM)] * 2,
        out_specs=(pl.BlockSpec(memory_space=pltpu.VMEM),) * 2,
        scratch_shapes=[
            pltpu.VMEM((2, CHUNKS, 2, HALF, local // CHUNKS), jnp.float32),
            pltpu.VMEM((CHUNKS, 2, HALF, local // CHUNKS), jnp.float32),
            pltpu.VMEM((2, INNER, 8, LANES), jnp.float32),
            pltpu.VMEM((2, groups, 8, LANES), jnp.float32),
            pltpu.SemaphoreType.DMA((2, INNER)),
            pltpu.SemaphoreType.DMA((2, INNER)),
            pltpu.SemaphoreType.DMA((2, groups)),
            pltpu.SemaphoreType.DMA((2, groups)),
            pltpu.SemaphoreType.DMA((2, CHUNKS)),
            pltpu.SemaphoreType.DMA((2, 2, CHUNKS)),
        ],
        compiler_params=pltpu.CompilerParams(collective_id=0, has_side_effects=True),
        name="rounds",
    )(snapshots, step_table(plan))
    return field * field, energy[0, :WIDTH] / (local * cells)


def solution(mesh):
    return jax.shard_map(
        on_device,
        mesh=mesh,
        in_specs=(P("blk", "cell"), P()),
        out_specs=(P("blk", "cell"), P("blk")),
        check_vma=False,
    )
```

time: 170 us -> 175 us (1.029)
  local copies, waits for them, and re-layouts: 0.08 us -> 8.01 us
  Pallas kernels: 165 us -> 163 us
    gather x0 -> x3, local copies, waits for them, and re-layouts: none -> 7.2 us  [step_table(): both = jnp.take_along_axis(plan, following, axis=1)]
    pallas_call x1, Pallas kernels: 165 us -> 163 us  [on_device(): pl.pallas_call(functools.partial(kernel, groups, blocks), out_shape=(jax....]
where the time goes in v2:
time: 175 us
  Pallas kernels  163 us (93%)
  local copies, waits for them, and re-layouts  8.01 us (5%)
  other arithmetic  3.01 us (2%)
    pallas_call x1, Pallas kernels, on_device(): pl.pallas_call(functools.partial(kernel, groups, blocks), out_shape=(jax....  163 us
    gather x3, local copies, waits for them, and re-layouts, step_table(): both = jnp.take_along_axis(plan, following, axis=1)  7.2 us

profile of v2, /device:TPU:1, one launch (start us, length us, event | category | flops | bytes accessed | tf_op | source)
XLA Modules:
  0.0 174.5 jit_solution(8196673894154553807)
XLA Ops:
  0.6 0.0 copy-start
  0.7 0.7 copy-done
  1.4 0.1 reshape.86
  1.4 7.1 %gather_fusion = s32[992]{0:T(1024)S(1)} fusion(s32[31,32]{1,0:T(8,128)S(1)} %copy-done, s32[992]{0:T(1024)S(1)} %reshape.86), kind=kCustom, calls=%fused_computation | custom fusion | bytes 15872 | tf_op jit(solution)/shard_map/jit(take_along_axis)/gather | solution.py:108
  8.5 0.1 reshape.89
  8.6 0.1 tile.10
  8.7 0.7 pad_add_fusion.plan_ref
  9.4 162.8 %rounds.1 = (f32[32,2048]{1,0:T(8,128)}, f32[1,128]{1,0:T(1,128)}) custom-call(f32[32,2048]{1,0:T(8,128)} %snap_ref.1, s32[64,128]{1,0:T(8,128)} %pad_add_fusion.plan_ref), custom_call_target="tpu_custom_call" | custom-call | tf_op jit(solution)/shard_map/rounds/pallas_call | solution.py:266
  172.2 0.0 copy-start.1
  172.2 1.8 %mul.3 = f32[32,2048]{1,0:T(8,128)} multiply(f32[32,2048]{1,0:T(8,128)} %get-tuple-element.4, f32[32,2048]{1,0:T(8,128)} %get-tuple-element.4) | non-fusion elementwise | flops 65536 | bytes 786432 | tf_op jit(solution)/shard_map/mul | solution.py:287
  174.0 0.0 copy-done.1
  174.0 0.5 multiply_bitcast_fusion
  (8 shorter events, 0.1 us)
Async XLA Ops:
  0.6 0.7 copy-start
  172.2 1.8 %copy-start.1 = (f32[1,128]{1,0:T(1,128)S(1)}, f32[1,128]{1,0:T(1,128)}, u32[]{:S(2)}) copy-start(f32[1,128]{1,0:T(1,128)} %get-tuple-element.5) | copy-start | bytes 1540

commit v3 on v2

--- a/solution.py
+++ b/solution.py
@@ -8,7 +8,7 @@
 from jax.sharding import PartitionSpec as P
 
 ROUNDS = 7
-INNER = 8
+INNER = 2
 WIDTH = 32
 HALF = 16
 LANES = 128
@@ -60,6 +60,11 @@
     def to_front(value, group):
         return pltpu.roll(value, LANES - WIDTH * group, 1)
 
+    upper_rows = lax.broadcasted_iota(jnp.int32, (8, LANES), 0) < 4
+
+    def two_rows(first, second):
+        return jnp.where(upper_rows, jnp.broadcast_to(first, (8, LANES)), jnp.broadcast_to(second, (8, LANES)))
+
     def step(k, state):
         gram, turning, own, other, cross = state
         table = table_ref[pl.ds(k, 1), :]
@@ -69,21 +74,21 @@
         crossed = permuted(gram, index)
         from_own = at_mask(any_own_mask, crossed)
         from_partner = at_mask(partner_mask, crossed)
-        next_row = jnp.broadcast_to(to_front(table, 1), (8, LANES))
-
-        def at_next(value):
-            return permuted(jnp.broadcast_to(value, (8, LANES)), next_row)[:1]
-
-        own_q, own_pq = to_front(from_own, 1), to_front(from_own, 2)
-        partner_q, partner_pq = to_front(from_partner, 1), to_front(from_partner, 2)
-        both_own = 0.5 * (own_q + at_next(own_q))
-        both_partner = 0.5 * (partner_pq + at_next(partner_pq))
-        ahead = 0.5 * (own_pq + at_next(partner_q))
-        behind = 0.5 * (partner_q + at_next(own_pq))
+        next_row = jnp.broadcast_to(table_ref[pl.ds(k + 2 * WIDTH, 1), :], (8, LANES))
+        stack = two_rows(from_own, from_partner)
+        at_q, at_pq = to_front(stack, 1), to_front(stack, 2)
+        next_q, next_pq = permuted(stack, next_row + WIDTH), permuted(stack, next_row + 2 * WIDTH)
+        own_q, partner_q = at_q[:1], at_q[4:5]
+        own_pq, partner_pq = at_pq[:1], at_pq[4:5]
+        both_own = 0.5 * (own_q + next_q[:1])
+        both_partner = 0.5 * (partner_pq + next_pq[4:5])
+        ahead = 0.5 * (own_pq + next_q[4:5])
+        behind = 0.5 * (partner_q + next_pq[:1])
         cosine, sine = turn_of(own, other, cross, lane_row < table)
-        cosine_q, sine_q = at_next(cosine), at_next(sine)
+        next_turn = permuted(two_rows(cosine, sine), next_row)
+        cosine_q, sine_q = next_turn[:1], next_turn[4:5]
         next_own = own + sine * (2.0 * cosine * cross - sine * (own - other))
-        next_other = at_next(next_own)
+        next_other = permuted(jnp.broadcast_to(next_own, (8, LANES)), next_row)[:1]
         next_cross = (((cosine * cosine_q) * both_own + (sine * sine_q) * both_partner)
                       + ((cosine * sine_q) * ahead + (sine * cosine_q) * behind))
         half_done = gram * cosine + crossed * sine
@@ -109,7 +114,8 @@
     still = jnp.broadcast_to(same, plan.shape)
     table = jnp.concatenate([plan, following, both, still], axis=1)
     blank = jnp.zeros((1, LANES), jnp.int32)
-    return jnp.concatenate([table, blank, jnp.tile(plan, (1, LANES // WIDTH)), blank], axis=0)
+    return jnp.concatenate([table, blank, jnp.tile(plan, (1, LANES // WIDTH)), blank,
+                            jnp.tile(following, (1, LANES // WIDTH)), blank], axis=0)
 
 
 def kernel(groups, blocks, snap_ref, plan_ref, out_ref, mode_ref,

time: 175 us -> 163 us (0.931)
  Pallas kernels: 163 us -> 146 us
  local copies, waits for them, and re-layouts: 8.01 us -> 13.8 us
    pallas_call x1, Pallas kernels: 163 us -> 146 us  [on_device(): pl.pallas_call(functools.partial(kernel, groups, blocks), out_shape=(jax....]
    concatenate x0 -> x1, local copies, waits for them, and re-layouts: none -> 5.68 us  [step_table(): jnp.concatenate([table, blank, jnp.tile(plan, (1, LANES // WIDTH)), blank...]
where the time goes in v3:
time: 163 us; the launch traced here: 162 us
  Pallas kernels  146 us (90%)
  local copies, waits for them, and re-layouts  13.8 us (8%)
  other arithmetic  2.39 us (1%)
    pallas_call x1, Pallas kernels, on_device(): pl.pallas_call(functools.partial(kernel, groups, blocks), out_shape=(jax....  146 us
    gather x3, local copies, waits for them, and re-layouts, step_table(): both = jnp.take_along_axis(plan, following, axis=1)  7.2 us
    concatenate x1, local copies, waits for them, and re-layouts, step_table(): jnp.concatenate([table, blank, jnp.tile(plan, (1, LANES // WIDTH)), blank...  5.68 us

profile of v3, /device:TPU:1, one launch (start us, length us, event | category | flops | bytes accessed | tf_op | source)
XLA Modules:
  0.0 162.4 jit_solution(4975656305888212520)
XLA Ops:
  0.6 0.0 copy-start
  0.7 0.7 copy-done
  1.4 0.1 reshape.90
  1.4 7.1 %gather_fusion = s32[992]{0:T(1024)S(1)} fusion(s32[31,32]{1,0:T(8,128)S(1)} %copy-done, s32[992]{0:T(1024)S(1)} %reshape.90), kind=kCustom, calls=%fused_computation | custom fusion | bytes 15872 | tf_op jit(solution)/shard_map/jit(take_along_axis)/gather | solution.py:113
  8.5 0.1 reshape.93
  8.6 0.1 pad_add_fusion.1
  8.7 0.1 tile.21
  8.8 0.1 tile.9
  8.9 5.7 %concatenate.38.plan_ref = s32[96,128]{1,0:T(8,128)} concatenate(s32[31,128]{1,0:T(8,128)S(1)} %pad_add_fusion.1, s32[1,128]{1,0:T(1,128)S(1)} %broadcast_in_dim.13, s32[31,128]{1,0:T(8,128)S(1)} %tile.9, s32[1,128]{1,0:T(1,128)S(1)} %broadcast_in_dim.13, s32[31,128]{1,0:T(8,128)S(1)} %tile.21, s32[1,128]{1,0:T(1,128)S(1)} %broadcast_in_dim.13), dimensions={0} | concatenate | bytes 98304 | tf_op jit(solution)/shard_map/concatenate | solution.py:117
  14.6 145.5 %rounds.1 = (f32[32,2048]{1,0:T(8,128)}, f32[1,128]{1,0:T(1,128)}) custom-call(f32[32,2048]{1,0:T(8,128)} %snap_ref.1, s32[96,128]{1,0:T(8,128)} %concatenate.38.plan_ref), custom_call_target="tpu_custom_call" | custom-call | tf_op jit(solution)/shard_map/rounds/pallas_call | solution.py:272
  160.1 0.0 copy-start.1
  160.1 1.8 %mul.3 = f32[32,2048]{1,0:T(8,128)} multiply(f32[32,2048]{1,0:T(8,128)} %get-tuple-element.4, f32[32,2048]{1,0:T(8,128)} %get-tuple-element.4) | non-fusion elementwise | flops 65536 | bytes 786432 | tf_op jit(solution)/shard_map/mul | solution.py:293
  161.9 0.0 copy-done.1
  161.9 0.5 multiply_bitcast_fusion
  (9 shorter events, 0.1 us)
Async XLA Ops:
  0.6 0.7 copy-start
  160.1 1.8 %copy-start.1 = (f32[1,128]{1,0:T(1,128)S(1)}, f32[1,128]{1,0:T(1,128)}, u32[]{:S(2)}) copy-start(f32[1,128]{1,0:T(1,128)} %get-tuple-element.5) | copy-start | bytes 1540

commit v4 on v3

--- a/solution.py
+++ b/solution.py
@@ -12,7 +12,7 @@
 WIDTH = 32
 HALF = 16
 LANES = 128
-CHUNKS = 4
+CHUNKS = 2
 MESH = pl.DeviceIdType.MESH
 HIGHEST = lax.Precision.HIGHEST
 

time: 163 us -> 166 us (1.018)
  Pallas kernels: 146 us -> 148 us
    pallas_call x1, Pallas kernels: 146 us -> 148 us  [on_device(): pl.pallas_call(functools.partial(kernel, groups, blocks), out_shape=(jax....]
where the time goes in v4:
time: 166 us; the launch traced here: 165 us
  Pallas kernels  148 us (89%)
  local copies, waits for them, and re-layouts  13.8 us (8%)
  other arithmetic  2.39 us (1%)
    pallas_call x1, Pallas kernels, on_device(): pl.pallas_call(functools.partial(kernel, groups, blocks), out_shape=(jax....  148 us
    gather x3, local copies, waits for them, and re-layouts, step_table(): both = jnp.take_along_axis(plan, following, axis=1)  7.2 us
    concatenate x1, local copies, waits for them, and re-layouts, step_table(): jnp.concatenate([table, blank, jnp.tile(plan, (1, LANES // WIDTH)), blank...  5.68 us

profile of v4, /device:TPU:1, one launch (start us, length us, event | category | flops | bytes accessed | tf_op | source)
XLA Modules:
  0.0 165.1 jit_solution(5609999941062099340)
XLA Ops:
  0.6 0.0 copy-start
  0.7 0.7 copy-done
  1.4 0.1 reshape.90
  1.4 7.1 %gather_fusion = s32[992]{0:T(1024)S(1)} fusion(s32[31,32]{1,0:T(8,128)S(1)} %copy-done, s32[992]{0:T(1024)S(1)} %reshape.90), kind=kCustom, calls=%fused_computation | custom fusion | bytes 15872 | tf_op jit(solution)/shard_map/jit(take_along_axis)/gather | solution.py:113
  8.5 0.1 reshape.93
  8.6 0.1 pad_add_fusion.1
  8.7 0.1 tile.21
  8.8 0.1 tile.9
  8.9 5.7 %concatenate.38.plan_ref = s32[96,128]{1,0:T(8,128)} concatenate(s32[31,128]{1,0:T(8,128)S(1)} %pad_add_fusion.1, s32[1,128]{1,0:T(1,128)S(1)} %broadcast_in_dim.13, s32[31,128]{1,0:T(8,128)S(1)} %tile.9, s32[1,128]{1,0:T(1,128)S(1)} %broadcast_in_dim.13, s32[31,128]{1,0:T(8,128)S(1)} %tile.21, s32[1,128]{1,0:T(1,128)S(1)} %broadcast_in_dim.13), dimensions={0} | concatenate | bytes 98304 | tf_op jit(solution)/shard_map/concatenate | solution.py:117
  14.6 148.2 %rounds.1 = (f32[32,2048]{1,0:T(8,128)}, f32[1,128]{1,0:T(1,128)}) custom-call(f32[32,2048]{1,0:T(8,128)} %snap_ref.1, s32[96,128]{1,0:T(8,128)} %concatenate.38.plan_ref), custom_call_target="tpu_custom_call" | custom-call | tf_op jit(solution)/shard_map/rounds/pallas_call | solution.py:272
  162.8 0.0 copy-start.1
  162.8 1.8 %mul.3 = f32[32,2048]{1,0:T(8,128)} multiply(f32[32,2048]{1,0:T(8,128)} %get-tuple-element.4, f32[32,2048]{1,0:T(8,128)} %get-tuple-element.4) | non-fusion elementwise | flops 65536 | bytes 786432 | tf_op jit(solution)/shard_map/mul | solution.py:293
  164.6 0.0 copy-done.1
  164.6 0.5 multiply_bitcast_fusion
  (9 shorter events, 0.1 us)
Async XLA Ops:
  0.6 0.7 copy-start
  162.8 1.8 %copy-start.1 = (f32[1,128]{1,0:T(1,128)S(1)}, f32[1,128]{1,0:T(1,128)}, u32[]{:S(2)}) copy-start(f32[1,128]{1,0:T(1,128)} %get-tuple-element.5) | copy-start | bytes 1540
